TPU v7x, 128 devices: a whole 4x4x4 slice. The times are simulated.
128 devices in a mesh: req: 8 (over x, y_hi), hid: 16 (over y_lo, z, core).
Axes of the slice: x: 4, y: 4 (y_hi: 2, y_lo: 2; y = y_hi * 2 + y_lo), z: 4, core: 2. Of those that a mesh axis runs over, the one named last changes fastest.
Arguments:
- input_activations: bfloat16 [8, 512, 4096], P('req'), may hold values from -6 to 6
- prompt_extents: int32 [8], P('req'), may hold values from 1 to 512, as said below
- continuing_flags: int32 [8], P('req'), may hold values from 0 to 1, as said below
- owning_index: int32 [8], P('req'), may hold values from 0 to 15
- partition_arrangement: int32 [128], replicated, may hold values from 0 to 127, each once
- training_accept_pieces: float32 [4096, 4096], P(('req', 'hid')), may hold values from -0.09375 to 0.09375
- training_lookup_pieces: float32 [4096, 4096], P(('req', 'hid')), may hold values from -0.09375 to 0.09375
- training_content_pieces: float32 [4096, 4096], P(('req', 'hid')), may hold values from -0.09375 to 0.09375
- normalizer_scales: bfloat16 [2, 4096], replicated, may hold values from 0.5 to 1.5
- prior_step_blends: bfloat16 [7, 4096], replicated, may hold values from 0.049804688 to 0.94921875
- forgetting_bias_vector: float32 [4096], P('hid'), may hold values from -7 to -3
- forgetting_left_lowrank: bfloat16 [4096, 128], replicated, may hold values from -0.09375 to 0.09375
- forgetting_right_lowrank: bfloat16 [128, 4096], P(None, 'hid'), may hold values from -0.5 to 0.5
- instant_emphasis: float32 [4096], P('hid'), may hold values from -3 to 3
- group_normalizer_scale: float32 [4096], P('hid'), may hold values from 0.5 to 1.5
- gating_projection: bfloat16 [4096, 4096], P(None, 'hid'), may hold values from -0.09375 to 0.09375
- mixing_exit_projection: bfloat16 [4096, 4096], P('hid'), may hold values from -0.09375 to 0.09375
- kept_summary_places: float32 [8, 16, 64, 64, 64], P('req', 'hid'), may hold values from -6 to 6
- previous_normed_entries: bfloat16 [8, 2, 4096], P('req'), may hold values from -6 to 6
- feedforward_entry_proj: bfloat16 [14336, 4096], P(('req', 'hid')), may hold values from -0.09375 to 0.09375
- feedforward_exit_proj: bfloat16 [14336, 4096], P(('req', 'hid')), may hold values from -0.046875 to 0.046875
- feedforward_accept_proj: bfloat16 [4096, 4096], P(None, 'hid'), may hold values from -0.09375 to 0.09375
Outputs:
- layer_out: bfloat16 [8, 512, 4096], P('req', None, 'hid')
- new_states: float32 [8, 64, 64, 64], P('req', 'hid')
- new_shift: bfloat16 [8, 2, 4096], P('req')
Inputs may be any that keep to these rules, and one draw needn't show every extreme that they name: `prompt_extents`: in every draw some request has length 512. `continuing_flags`: at least one request has 1 and at least one has 0. `owning_index`: read only where continuing_flags is 1. `partition_arrangement`: each of 0 to 127 appears once.
All inputs are finite; a program needn't handle non-finite values.
Results may differ from a plain program's by a relative error of at most 0.02.
Values may be sent and summed in bfloat16 or wider, within the bound.
A program may use at most 192 MiB of HBM per device.

v0:
```python
from functools import partial
import jax
import jax.numpy as jnp
from jax import lax
from jax.sharding import PartitionSpec as P

GROUP_DIMENSION = 64


def layer_norm(values, gain):
    center = values - jnp.mean(values, axis=-1, keepdims=True)
    spread = jnp.mean(center * center, axis=-1, keepdims=True)
    return center / jnp.sqrt(spread + 1e-05) * gain


def head_norm(outputs, gain_rows):
    center = outputs - jnp.mean(outputs, axis=-1, keepdims=True)
    spread = jnp.mean(center * center, axis=-1, keepdims=True)
    return center / jnp.sqrt(spread + 0.00064) * gain_rows


def shifted(values, first_row):
    return jnp.concatenate([first_row[None, :], values[:-1]], axis=0)


def segment_step(extra_diagonal_term, carried_summary, piece_sequence):
    acceptance_vectors, present_lookup_vectors, content_vectors, decays = piece_sequence
    inclusive = jnp.cumsum(decays, axis=0)
    exclusive = inclusive - decays
    closing = inclusive[-1]
    resulting_activations = jnp.einsum(
        "thi,hij->thj",
        acceptance_vectors * jnp.exp(exclusive),
        carried_summary,
        precision=lax.Precision.HIGHEST,
    )
    distance = exclusive[:, None] - inclusive[None, :]
    sizing = decays.shape[0]
    earlier = (jnp.arange(sizing)[:, None] > jnp.arange(sizing)[None, :]).astype(jnp.float32)
    factor = jnp.exp(jnp.minimum(distance, 0.0)) * earlier[:, :, None, None]
    scores = jnp.sum(
        acceptance_vectors[:, None] * factor * present_lookup_vectors[None, :], axis=-1
    )
    resulting_activations = resulting_activations + jnp.einsum(
        "tsh,shj->thj", scores, content_vectors, precision=lax.Precision.HIGHEST
    )
    resulting_activations = (
        resulting_activations
        + jnp.sum(
            acceptance_vectors * extra_diagonal_term * present_lookup_vectors,
            axis=-1,
            keepdims=True,
        )
        * content_vectors
    )
    weighted = present_lookup_vectors * jnp.exp(closing[None] - inclusive)
    carried_summary = jnp.exp(closing)[:, :, None] * carried_summary + jnp.einsum(
        "shi,shj->hij", weighted, content_vectors, precision=lax.Precision.HIGHEST
    )
    return (carried_summary, resulting_activations)


def local(
    input_activations,
    prompt_extents,
    continuing_flags,
    owning_index,
    partition_arrangement,
    training_accept_pieces,
    training_lookup_pieces,
    training_content_pieces,
    normalizer_scales,
    prior_step_blends,
    forgetting_bias_vector,
    forgetting_left_lowrank,
    forgetting_right_lowrank,
    instant_emphasis,
    group_normalizer_scale,
    gating_projection,
    mixing_exit_projection,
    kept_summary_places,
    previous_normed_entries,
    feedforward_entry_proj,
    feedforward_exit_proj,
    feedforward_accept_proj,
):
    token_rows = input_activations[0]
    seq_len, width = token_rows.shape
    local_width = mixing_exit_projection.shape[0]
    groups_on_device = local_width // GROUP_DIMENSION
    shards = partition_arrangement.shape[0]
    shard_rows = width // shards
    length = prompt_extents[0]
    resuming = continuing_flags[0]
    present = jnp.arange(seq_len) < length
    gain_rows = normalizer_scales.astype(jnp.float32)
    mix_rows = prior_step_blends.astype(jnp.float32)
    carried = previous_normed_entries[0].astype(jnp.float32)
    normed_in = layer_norm(token_rows.astype(jnp.float32), gain_rows[0])
    before = shifted(normed_in, jnp.where(resuming == 1, carried[0], 0.0))
    blended = (normed_in[None] + (before - normed_in)[None] * mix_rows[:5, None, :]).astype(
        jnp.bfloat16
    )
    permuted = jnp.take(
        blended[:3].reshape(3, seq_len, shards, shard_rows), partition_arrangement, axis=2
    ).reshape(3, seq_len, width)
    local_rows = jnp.stack(
        [training_accept_pieces, training_lookup_pieces, training_content_pieces]
    ).astype(jnp.bfloat16)
    collected = lax.all_gather(local_rows, "req", axis=1, tiled=True)
    swapped = lax.all_to_all(collected, "hid", split_axis=2, concat_axis=1, tiled=True)
    hid_count = lax.axis_size("hid")
    req_count = lax.axis_size("req")
    ordered = (
        swapped.reshape(3, hid_count, req_count, shard_rows, local_width)
        .transpose(0, 2, 1, 3, 4)
        .reshape(3, width, local_width)
    )
    projected = jnp.einsum("mtd,mdc->mtc", permuted, ordered, preferred_element_type=jnp.float32)
    low_rank = jnp.tanh(
        jnp.dot(blended[3], forgetting_left_lowrank, preferred_element_type=jnp.float32)
    ).astype(jnp.bfloat16)
    log_decay = -jnp.exp(
        forgetting_bias_vector
        + jnp.dot(low_rank, forgetting_right_lowrank, preferred_element_type=jnp.float32)
    )
    log_decay = jnp.where(present[:, None], log_decay, 0.0)
    gate = jax.nn.silu(jnp.dot(blended[4], gating_projection, preferred_element_type=jnp.float32))
    present_lookup_vectors = jnp.where(present[:, None], projected[1], 0.0)
    fetched = lax.all_to_all(
        kept_summary_places.astype(jnp.bfloat16), "hid", split_axis=2, concat_axis=1, tiled=True
    ).astype(kept_summary_places.dtype)
    chosen = lax.dynamic_index_in_dim(fetched[0], owning_index[0], 0, keepdims=False)
    carried_summary = jnp.where(resuming == 1, chosen, 0.0)
    block_len = min(64, seq_len)
    count_blocks = seq_len // block_len

    def by_blocks(values):
        return values.reshape(count_blocks, block_len, groups_on_device, GROUP_DIMENSION)

    sequences = (
        by_blocks(projected[0]),
        by_blocks(present_lookup_vectors),
        by_blocks(projected[2]),
        by_blocks(log_decay),
    )
    segment_cursor = partial(
        segment_step, instant_emphasis.reshape(groups_on_device, GROUP_DIMENSION)
    )
    carried_summary, outputs = lax.scan(segment_cursor, carried_summary, sequences)
    outputs = outputs.reshape(seq_len, groups_on_device, GROUP_DIMENSION)
    grouped = head_norm(
        outputs, group_normalizer_scale.reshape(groups_on_device, GROUP_DIMENSION)
    ).reshape(seq_len, local_width)
    gated = (grouped * gate).astype(jnp.bfloat16)
    head_terms = jnp.dot(gated, mixing_exit_projection, preferred_element_type=jnp.float32)
    attended = lax.psum(head_terms.astype(jnp.bfloat16), "hid").astype(jnp.float32)
    middle = (token_rows.astype(jnp.float32) + attended).astype(jnp.bfloat16)
    mid_share = lax.dynamic_slice_in_dim(
        middle, lax.axis_index("hid") * local_width, local_width, 1
    )
    chan_in = layer_norm(middle.astype(jnp.float32), gain_rows[1])
    chan_before = shifted(chan_in, jnp.where(resuming == 1, carried[1], 0.0))
    chan_mixed = (chan_in[None] + (chan_before - chan_in)[None] * mix_rows[5:, None, :]).astype(
        jnp.bfloat16
    )
    key_rows = lax.all_gather(feedforward_entry_proj, "req", axis=0, tiled=True)
    value_rows = lax.all_gather(feedforward_exit_proj, "req", axis=0, tiled=True)
    inner = lax.dot_general(
        chan_mixed[0], key_rows, (((1,), (1,)), ((), ())), preferred_element_type=jnp.float32
    )
    hidden = jnp.square(jnp.maximum(inner, 0.0)).astype(jnp.bfloat16)
    channel_terms = jnp.dot(hidden, value_rows, preferred_element_type=jnp.float32)
    mixed_out = lax.psum_scatter(
        channel_terms.astype(jnp.bfloat16), "hid", scatter_dimension=1, tiled=True
    ).astype(jnp.float32)
    gate_rows = jax.nn.sigmoid(
        jnp.dot(chan_mixed[1], feedforward_accept_proj, preferred_element_type=jnp.float32)
    )
    combined = mid_share.astype(jnp.float32) + gate_rows * mixed_out
    layer_out = jnp.where(present[:, None], combined, 0.0).astype(jnp.bfloat16)[None]
    last_index = length - 1
    shift_out = jnp.stack(
        [
            lax.dynamic_index_in_dim(normed_in, last_index, 0, keepdims=False),
            lax.dynamic_index_in_dim(chan_in, last_index, 0, keepdims=False),
        ]
    ).astype(jnp.bfloat16)[None]
    return (layer_out, carried_summary[None], shift_out)


def solution(mesh):
    placed = (
        P("req", None, None),
        P("req"),
        P("req"),
        P("req"),
        P(),
        P(("req", "hid"), None),
        P(("req", "hid"), None),
        P(("req", "hid"), None),
        P(),
        P(),
        P("hid"),
        P(),
        P(None, "hid"),
        P("hid"),
        P("hid"),
        P(None, "hid"),
        P("hid", None),
        P("req", "hid", None, None, None),
        P("req", None, None),
        P(("req", "hid"), None),
        P(("req", "hid"), None),
        P(None, "hid"),
    )
    return jax.shard_map(
        local,
        mesh=mesh,
        in_specs=placed,
        out_specs=(P("req", None, "hid"), P("req", "hid", None, None), P("req", None, None)),
        check_vma=False,
    )
```

profile of v0, /device:TPU:6, one launch (start us, length us, event | category | flops | bytes accessed | tf_op | source)
XLA Modules:
  0.0 817.3 jit_solution(10165721648546910749)
XLA Ops:
  14.0 6.4 all-to-all-start
  21.3 3.4 convert_reduce_fusion
  24.8 3.4 fusion.19
  28.3 1.8 fusion.20
  30.1 4.1 slice_bitcast_fusion.1
  36.6 67.1 %all-gather.4.cloned.1.call-done = bf16[3,256,4096]{2,1,0:T(8,128)(2,1)} async-done(((bf16[3,32,4096]{2,1,0:T(8,128)(2,1)}), bf16[3,256,4096]{2,1,0:T(8,128)(2,1)}) %all-gather.4.cloned.1.call-update) | async-done | bytes 6291472 | tf_op jit(solution)/shard_map/all_gather | solution.py:110
  103.7 13.1 %copy.123 = bf16[3,256,4096]{1,0,2:T(4,128)(2,1)} copy(bf16[3,256,4096]{2,1,0:T(8,128)(2,1)} %all-gather.4.cloned.1.call-done) | data formatting | bytes 12582912 | tf_op jit(solution)/shard_map/all_gather | solution.py:110
  116.8 4.8 all-to-all-start.1
  121.9 10.4 %fusion.27 = (f32[512,4096]{1,0:T(8,128)}, f32[512,4096]{1,0:T(8,128)}) fusion(bf16[1,512,4096]{2,1,0:T(8,128)(2,1)} %param.24, f32[4096]{0:T(1024)S(1)} %bitcast.201, f32[512]{0:T(512)S(1)} %add_sqrt_fusion.1, f32[512]{0:T(512)S(1)} %broadcast_multiply_fusion.1, f32[1,511,4096]{2,1,0:T(8,128)} %slice_bitcast_fusion.1, f32[1,1,4096]{2,1,0:T(1,128)S(1)} %get-tuple-element.126), kind=kLoop, calls=%fused_computation.55 | loop fusion | flops 12582912 | bytes 29380608 | tf_op jit(solution)/shard_map/add | solution.py:101
  132.3 9.0 %copy.120 = f32[512,4096]{0,1:T(8,128)} copy(f32[512,4096]{1,0:T(8,128)} %get-tuple-element.120) | data formatting | bytes 16777216 | tf_op jit(solution)/shard_map/add | solution.py:101
  141.3 9.0 %copy.121 = f32[512,4096]{0,1:T(8,128)} copy(f32[512,4096]{1,0:T(8,128)} %get-tuple-element.121) | data formatting | bytes 16777216 | tf_op jit(solution)/shard_map/mul | solution.py:101
  150.4 10.3 %add_convert_fusion = bf16[5,512,4096]{1,2,0:T(8,128)(2,1)S(1)} fusion(f32[5,4096]{1,0:T(8,128)S(1)} %slice.75, f32[512,4096]{0,1:T(8,128)} %copy.121, f32[512,4096]{0,1:T(8,128)} %copy.120), kind=kLoop, calls=%fused_computation.28 | loop fusion | flops 31457280 | bytes 37830656 | tf_op jit(solution)/shard_map/convert_element_type | solution.py:101
  160.7 6.5 slice.77
  167.2 4.2 copy-done.4
  171.4 12.8 %gather_fusion = bf16[128,3,512,32]{2,3,1,0:T(8,128)(2,1)} fusion(bf16[3,512,128,32]{1,3,2,0:T(8,128)(2,1)} %bitcast.190, s32[1024]{0:T(1024)S(1)} %pad_clamp_fusion), kind=kCustom, calls=%fused_computation | custom fusion | bytes 25166336 | tf_op jit(solution)/shard_map/jit(_take)/gather | solution.py:104
  184.2 10.7 %copy.122 = bf16[3,512,128,32]{1,3,2,0:T(8,128)(2,1)} copy(bf16[3,512,128,32]{1,3,0,2:T(8,128)(2,1)} %bitcast.191) | data formatting | bytes 25165824 | tf_op jit(solution)/shard_map/jit(_take)/gather | solution.py:104
  195.8 3.9 fusion.34
  202.5 11.2 %bitcast_select_fusion = bf16[3,512,4096]{1,2,0:T(8,128)(2,1)} fusion(bf16[3,512,128,32]{1,3,2,0:T(8,128)(2,1)} %copy.122, pred[4096]{0:T(1024)(128)(4,1)S(1)} %broadcast_in_dim.95), kind=kLoop, calls=%fused_computation.30 | loop fusion | flops 6291456 | bytes 25169920 | tf_op jit(solution)/shard_map/jit(_take)/select_n | solution.py:104
  216.2 27.1 %all-to-all-done.1 = bf16[3,256,4096]{1,0,2:T(4,128)(2,1)} async-done(((bf16[3,256,4096]{1,0,2:T(4,128)(2,1)}), bf16[3,256,4096]{1,0,2:T(4,128)(2,1)}, u32[]{:S(2)}, u32[]{:S(2)}) %all-to-all-start.1) | async-done | bytes 6291488 | tf_op jit(solution)/shard_map/all_to_all | solution.py:111
  243.3 6.9 copy.124
  250.2 9.1 %copy.125 = bf16[3,16,256,256]{3,2,1,0:T(8,128)(2,1)} copy(bf16[3,16,256,256]{2,3,1,0:T(8,128)(2,1)} %bitcast.193) | data formatting | bytes 12582912 | tf_op jit(solution)/shard_map/all_to_all | solution.py:111
  259.3 6.5 copy.126
  265.7 12.0 %fusion.61 = f32[3,512,256]{2,1,0:T(8,128)} fusion(bf16[3,512,4096]{1,2,0:T(8,128)(2,1)} %bitcast_select_fusion, bf16[3,4096,256]{2,1,0:T(8,128)(2,1)} %bitcast.196), kind=kOutput, calls=%fused_computation.119 | convolution fusion | flops 3221225472 | bytes 20447232 | tf_op jit(solution)/shard_map/mtd,mdc->mtc/dot_general | solution.py:119
  277.7 2.6 fusion.58
  281.7 2.5 reshape_squeeze.6
  284.2 2.4 reshape_squeeze.7
  288.1 79.8 %while.12 = (s32[]{:T(128)}, f32[4,64,64]{2,1,0:T(8,128)S(1)}, f32[8,64,4,64]{3,1,2,0:T(8,128)}, f32[8,64,4,64]{3,2,1,0:T(4,128)}, f32[8,64,4,64]{3,2,1,0:T(4,12...) while((s32[]{:T(128)}, f32[4,64,64]{2,1,0:T(8,128)S(1)}, ...), condition=%wide.region_6.7_spmd, body=%wide.region_2.6_spmd.sunk | while | flops 45260544 | bytes 2537577 | solution.py:150
  292.0 3.4 multiply_reduce_fusion.6
  302.0 3.4 multiply_reduce_fusion.6
  311.9 3.4 multiply_reduce_fusion.6
  321.9 3.4 multiply_reduce_fusion.6
  331.8 3.4 multiply_reduce_fusion.6
  341.8 3.4 multiply_reduce_fusion.6
  351.7 3.4 multiply_reduce_fusion.6
  361.7 3.4 multiply_reduce_fusion.6
  367.9 2.0 copy.130
  372.9 1.9 multiply_reduce_fusion.2
  376.3 9.6 %convolution_convert_fusion.1 = bf16[512,4096]{1,0:T(8,128)(2,1)} fusion(bf16[256,4096]{1,0:T(8,128)(2,1)S(1)} %copy-done, bf16[4096,256]{1,0:T(8,128)(2,1)} %param.39, bf16[5,512,4096]{1,2,0:T(8,128)(2,1)} %copy-done.4, f32[512,256]{1,0:T(8,128)S(1)} %copy.135, f32[512,256]{1,0:T(8,128)} %reshape.249, f32[512,256]{1,0:T(8,128)} %copy.132, ...), kind=kOutput, calls=%fused_computation.54 | convolution fusion | flops 2150760448 | bytes 14156800 | tf_op jit(solution)/shard_map/dot_general | solution.py:156
  387.2 135.4 %all-reduce.2.cloned.1.call-done = bf16[512,4096]{1,0:T(8,128)(2,1)} async-done(((bf16[512,4096]{1,0:T(8,128)(2,1)}), bf16[512,4096]{1,0:T(8,128)(2,1)}) %all-reduce.2.cloned.1.call-update) | async-done | bytes 4194320 | tf_op jit(solution)/shard_map/psum | solution.py:157
  522.7 5.2 convert_reduce_fusion.1
  529.1 2.1 fusion.22
  531.2 3.5 maximum_subtract_fusion.1
  534.7 4.8 add_convert_fusion.1
  539.5 83.5 %all-gather.6.cloned.1.call-done = bf16[896,4096]{1,0:T(8,128)(2,1)} async-done(((bf16[112,4096]{1,0:T(8,128)(2,1)}), bf16[896,4096]{1,0:T(8,128)(2,1)}) %all-gather.6.cloned.1.call-update) | async-done | bytes 7340048 | tf_op jit(solution)/shard_map/all_gather | solution.py:167
  623.0 99.4 %all-gather.8.cloned.1.call-done = bf16[896,4096]{1,0:T(8,128)(2,1)} async-done(((bf16[112,4096]{1,0:T(8,128)(2,1)}), bf16[896,4096]{1,0:T(8,128)(2,1)}) %all-gather.8.cloned.1.call-update) | async-done | bytes 7340048 | tf_op jit(solution)/shard_map/all_gather | solution.py:168
  722.4 16.2 %convolution_convert_fusion = bf16[512,4096]{1,0:T(8,128)(2,1)} fusion(bf16[896,4096]{1,0:T(8,128)(2,1)} %all-gather.8.cloned.1.call-done, bf16[896,4096]{1,0:T(8,128)(2,1)} %all-gather.6.cloned.1.call-done, bf16[2,512,4096]{2,1,0:T(8,128)(2,1)} %add_convert_fusion.1), kind=kOutput, calls=%fused_computation.53 | convolution fusion | flops 7519666176 | bytes 23068672 | tf_op jit(solution)/shard_map/dot_general | solution.py:173
  741.1 64.5 %reduce-scatter.2.cloned.1.call-done = bf16[512,256]{1,0:T(8,128)(2,1)} async-done(((bf16[512,4096]{1,0:T(8,128)(2,1)}), bf16[512,256]{1,0:T(8,128)(2,1)}) %reduce-scatter.2.cloned.1.call-update) | async-done | bytes 262160 | tf_op jit(solution)/shard_map/reduce_scatter | solution.py:174
  805.6 4.9 fusion.45
  (202 shorter events, 78.9 us)
Async XLA Ops:
  7.2 369.1 %copy-start = (bf16[256,4096]{1,0:T(8,128)(2,1)S(1)}, bf16[256,4096]{1,0:T(8,128)(2,1)}, u32[]{:S(2)}) copy-start(bf16[256,4096]{1,0:T(8,128)(2,1)} %param.40) | copy-start | bytes 6291460
  7.2 14.1 %copy-start.11 = (bf16[1,2,4096]{2,1,0:T(2,128)(2,1)S(1)}, bf16[1,2,4096]{2,1,0:T(2,128)(2,1)}, u32[]{:S(2)}) copy-start(bf16[1,2,4096]{2,1,0:T(2,128)(2,1)} %param.42) | copy-start | bytes 49156
  7.2 96.5 %all-gather.4.cloned.1.call-start = ((), (), s32[]{:S(2)}) async-start(), calls=%async_computation.3 | async-start | bytes 7077888 | tf_op jit(solution)/shard_map/all_gather | solution.py:110
  9.7 18.5 %copy-start.9 = (bf16[2,4096]{1,0:T(2,128)(2,1)S(1)}, bf16[2,4096]{1,0:T(2,128)(2,1)}, u32[]{:S(2)}) copy-start(bf16[2,4096]{1,0:T(2,128)(2,1)} %param.32) | copy-start | bytes 49156
  14.0 102.8 %all-to-all-start = ((bf16[16,2,8192]{2,1,0:T(2,128)(2,1)}), bf16[16,2,8192]{2,1,0:T(2,128)(2,1)S(1)}, u32[]{:S(2)}, u32[]{:S(2)}) async-start(bf16[16,2,8192]{2,1,0:T(2,128)(2,1)} %reshape.260), calls=%async_computation | async-start | bytes 1048576 | tf_op jit(solution)/shard_map/all_to_all | solution.py:130
  20.5 7.8 copy-start.1
  30.1 5.8 copy-start.5
  116.8 126.4 %all-to-all-start.1 = ((bf16[3,256,4096]{1,0,2:T(4,128)(2,1)}), bf16[3,256,4096]{1,0,2:T(4,128)(2,1)}, u32[]{:S(2)}, u32[]{:S(2)}) async-start(bf16[3,256,4096]{1,0,2:T(4,128)(2,1)} %copy.123), calls=%async_computation.1 | async-start | bytes 16777216 | tf_op jit(solution)/shard_map/all_to_all | solution.py:111
  121.6 401.1 %all-reduce.2.cloned.1.call-start = ((), (), s32[]{:S(2)}) async-start(), calls=%async_computation.4 | async-start | bytes 8388608 | tf_op jit(solution)/shard_map/psum | solution.py:157
  141.3 9.0 %copy-start.7 = (bf16[7,4096]{1,0:T(8,128)(2,1)S(1)}, bf16[7,4096]{1,0:T(8,128)(2,1)}, u32[]{:S(2)}) copy-start(bf16[7,4096]{1,0:T(8,128)(2,1)} %param.33) | copy-start | bytes 172036
  160.7 10.7 %copy-start.4 = (bf16[5,512,4096]{1,2,0:T(8,128)(2,1)}, bf16[5,512,4096]{1,2,0:T(8,128)(2,1)S(1)}, u32[]{:S(2)}) copy-start(bf16[5,512,4096]{1,2,0:T(8,128)(2,1)S(1)} %add_convert_fusion) | copy-start | bytes 62914564
  160.7 10.7 %copy-start.16 = (s32[128]{0:T(128)S(1)}, s32[128]{0:T(128)}, u32[]{:S(2)}) copy-start(s32[128]{0:T(128)} %param.28) | copy-start | bytes 1540
  184.2 11.6 %copy-start.13 = (bf16[128,256]{1,0:T(8,128)(2,1)S(1)}, bf16[128,256]{1,0:T(8,128)(2,1)}, u32[]{:S(2)}) copy-start(bf16[128,256]{1,0:T(8,128)(2,1)} %param.36) | copy-start | bytes 196612
  184.2 11.6 %copy-start.14 = (f32[256]{0:T(256)S(1)}, f32[256]{0:T(256)}, u32[]{:S(2)}) copy-start(f32[256]{0:T(256)} %param.34) | copy-start | bytes 3076
  195.8 17.8 %copy-start.17 = (pred[512]{0:T(512)(128)(4,1)}, pred[512]{0:T(512)(128)(4,1)S(1)}, u32[]{:S(2)}) copy-start(pred[512]{0:T(512)(128)(4,1)S(1)} %iota_compare_fusion.1) | copy-start | bytes 1540
  265.7 20.9 %copy-start.12 = (pred[8,64]{1,0:T(8,128)(4,1)S(1)}, pred[8,64]{1,0:T(8,128)(4,1)}, u32[]{:S(2)}) copy-start(pred[8,64]{1,0:T(8,128)(4,1)} %add_compare_fusion) | copy-start | bytes 1540
  367.9 18.0 %copy-start.6 = (f32[4,64,64]{2,1,0:T(8,128)}, f32[4,64,64]{2,1,0:T(8,128)S(1)}, u32[]{:S(2)}) copy-start(f32[4,64,64]{2,1,0:T(8,128)S(1)} %get-tuple-element.47) | copy-start | bytes 196612
  367.9 8.4 %copy-start.15 = (f32[256]{0:T(256)S(1)}, f32[256]{0:T(256)}, u32[]{:S(2)}) copy-start(f32[256]{0:T(256)} %param.38) | copy-start | bytes 3076
  376.3 11.0 %copy-start.8 = (bf16[7,4096]{1,0:T(8,128)(2,1)S(1)}, bf16[7,4096]{1,0:T(8,128)(2,1)}, u32[]{:S(2)}) copy-start(bf16[7,4096]{1,0:T(8,128)(2,1)} %param.33) | copy-start | bytes 172036
  385.8 237.2 %all-gather.6.cloned.1.call-start = ((), (), s32[]{:S(2)}) async-start(), calls=%async_computation.5 | async-start | bytes 8257536 | tf_op jit(solution)/shard_map/all_gather | solution.py:167
  386.6 335.8 %all-gather.8.cloned.1.call-start = ((), (), s32[]{:S(2)}) async-start(), calls=%async_computation.6 | async-start | bytes 8257536 | tf_op jit(solution)/shard_map/all_gather | solution.py:168
  387.2 418.5 %reduce-scatter.2.cloned.1.call-start = ((), (), s32[]{:S(2)}) async-start(), calls=%async_computation.7 | async-start | bytes 4456448 | tf_op jit(solution)/shard_map/reduce_scatter | solution.py:174
  527.8 3.4 copy-start.3
  527.8 3.4 copy-start.10
  531.2 3.5 copy-start.2
  539.5 266.1 %copy-start.18 = (pred[512]{0:T(512)(128)(4,1)S(1)}, pred[512]{0:T(512)(128)(4,1)}, u32[]{:S(2)}) copy-start(pred[512]{0:T(512)(128)(4,1)} %copy-done.17) | copy-start | bytes 1540
Sparse Core Ops, SparseCore 0:
  10.8 92.8 all-gather.3
  386.0 136.6 all-reduce.1
  525.0 97.9 all-gather.5
  625.2 97.1 all-gather.7
  738.7 66.8 reduce-scatter.1
where the time goes:
time: 824 us; the launch traced here: 817 us
  waiting for transfers between devices  478 us (58%)
  local copies, waits for them, and re-layouts  128 us (16%)
  other arithmetic  122 us (15%)
  matrix products  59.3 us (7%)
  between operations  16.6 us (2%)
  starting transfers between devices  11.7 us (1%)
    psum x1, waiting for transfers between devices, local(): lax.psum(head_terms.astype(jnp.bfloat16), 'hid').astype(jnp.float32)  135 us
    all_gather x1, waiting for transfers between devices, local(): lax.all_gather(feedforward_exit_proj, 'req', axis=0, tiled=True)  99.4 us
    all_gather x1, waiting for transfers between devices, local(): key_rows = lax.all_gather(feedforward_entry_proj, 'req', axis=0, tiled=True)  83.5 us
    all_gather x1, waiting for transfers between devices, local(): collected = lax.all_gather(local_rows, 'req', axis=1, tiled=True)  67.1 us
    reduce_scatter x1, waiting for transfers between devices, local(): lax.psum_scatter(channel_terms.astype(jnp.bfloat16), 'hid', scatter_dimen...  64.5 us
    all_to_all x1, waiting for transfers between devices, local(): lax.all_to_all(collected, 'hid', split_axis=2, concat_axis=1, tiled=True)  27.1 us
    reduce_sum x8, other arithmetic, segment_step(): jnp.sum(acceptance_vectors[:, None] * factor * present_lookup_vectors[Non...  27 us
    gather x2, local copies, waits for them, and re-layouts, local(): jnp.take(blended[:3].reshape(3, seq_len, shards, shard_rows), partition_a...  23.5 us
  transfers between devices with their start and end apart: 7, of which 6 were waited for; matrix products, arithmetic and copies ran while one was open for 17% of the time, Pallas kernels for 0%

commit v1 on v0

--- a/solution.py
+++ b/solution.py
@@ -108,7 +108,16 @@
         [training_accept_pieces, training_lookup_pieces, training_content_pieces]
     ).astype(jnp.bfloat16)
     collected = lax.all_gather(local_rows, "req", axis=1, tiled=True)
-    swapped = lax.all_to_all(collected, "hid", split_axis=2, concat_axis=1, tiled=True)
+    change_domain = lambda m, mesh_dim: jnp.concatenate(
+        lax.all_to_all(
+            jnp.stack(jnp.split(m, lax.axis_size(mesh_dim), 2), 0),
+            axis_name=mesh_dim,
+            split_axis=0,
+            concat_axis=0,
+        ),
+        1,
+    )
+    swapped = change_domain(collected, "hid")
     hid_count = lax.axis_size("hid")
     req_count = lax.axis_size("req")
     ordered = (

time: 824 us -> 791 us (0.960)
  waiting for transfers between devices: 478 us -> 444 us
    unnamed x40 -> x55, local copies, waits for them, and re-layouts: 9.24 us -> 37.5 us
    all_to_all x1, waiting for transfers between devices: 27.1 us -> 0.01 us  [local(): lax.all_to_all(jnp.stack(jnp.split(m, lax.axis_size(mesh_dim), 2), 0), ax...]
    all_to_all x2 -> x0, local copies, waits for them, and re-layouts: 16 us -> none  [local(): lax.all_to_all(collected, 'hid', split_axis=2, concat_axis=1, tiled=True)]
    all_gather x1 -> x0, local copies, waits for them, and re-layouts: 13.1 us -> none  [local(): collected = lax.all_gather(local_rows, 'req', axis=1, tiled=True)]
  transfers between devices with their start and end apart: 7 -> 7, of which waited for: 6 -> 5; matrix products, arithmetic and copies ran while one was open for 17% -> 20% of each run, Pallas kernels for 0% -> 0%
where the time goes in v1:
time: 791 us; the launch traced here: 784 us
  waiting for transfers between devices  444 us (56%)
  local copies, waits for them, and re-layouts  129 us (16%)
  other arithmetic  123 us (16%)
  matrix products  59.3 us (7%)
  between operations  16.6 us (2%)
  starting transfers between devices  11.6 us (1%)
    psum x1, waiting for transfers between devices, local(): lax.psum(head_terms.astype(jnp.bfloat16), 'hid').astype(jnp.float32)  129 us
    all_gather x1, waiting for transfers between devices, local(): lax.all_gather(feedforward_exit_proj, 'req', axis=0, tiled=True)  99.4 us
    all_gather x1, waiting for transfers between devices, local(): key_rows = lax.all_gather(feedforward_entry_proj, 'req', axis=0, tiled=True)  83.5 us
    all_gather x1, waiting for transfers between devices, local(): collected = lax.all_gather(local_rows, 'req', axis=1, tiled=True)  66 us
    reduce_scatter x1, waiting for transfers between devices, local(): lax.psum_scatter(channel_terms.astype(jnp.bfloat16), 'hid', scatter_dimen...  64.5 us
    unnamed x55, local copies, waits for them, and re-layouts  37.5 us
    reduce_sum x8, other arithmetic, segment_step(): jnp.sum(acceptance_vectors[:, None] * factor * present_lookup_vectors[Non...  27 us
    gather x2, local copies, waits for them, and re-layouts, local(): jnp.take(blended[:3].reshape(3, seq_len, shards, shard_rows), partition_a...  23.5 us
  transfers between devices with their start and end apart: 7, of which 5 were waited for; matrix products, arithmetic and copies ran while one was open for 20% of the time, Pallas kernels for 0%

profile of v1, /device:TPU:6, one launch (start us, length us, event | category | flops | bytes accessed | tf_op | source)
XLA Modules:
  0.0 784.0 jit_solution(63749274998826633)
XLA Ops:
  14.0 6.4 all-to-all-start
  21.3 3.4 convert_reduce_fusion
  24.7 3.4 fusion.19
  28.9 1.8 fusion.20
  30.7 3.3 copy-done.5
  34.0 3.8 slice_bitcast_fusion.1
  37.7 66.0 %all-gather.4.cloned.1.call-done = bf16[3,256,4096]{2,1,0:T(8,128)(2,1)} async-done(((bf16[3,32,4096]{2,1,0:T(8,128)(2,1)}), bf16[3,256,4096]{2,1,0:T(8,128)(2,1)}) %all-gather.4.cloned.1.call-update) | async-done | bytes 6291472 | tf_op jit(solution)/shard_map/all_gather | solution.py:110
  109.0 1.8 fusion.61
  121.4 1.8 fusion.54
  128.6 1.8 fusion.50
  132.2 4.7 all-to-all-start.1
  137.2 10.4 %fusion.27 = (f32[512,4096]{1,0:T(8,128)}, f32[512,4096]{1,0:T(8,128)}) fusion(bf16[1,512,4096]{2,1,0:T(8,128)(2,1)} %param.24, f32[4096]{0:T(1024)S(1)} %bitcast.262, f32[512]{0:T(512)S(1)} %add_sqrt_fusion.1, f32[512]{0:T(512)S(1)} %broadcast_multiply_fusion.1, f32[1,511,4096]{2,1,0:T(8,128)} %slice_bitcast_fusion.1, f32[1,1,4096]{2,1,0:T(1,128)S(1)} %get-tuple-element.118), kind=kLoop, calls=%fused_computation.55 | loop fusion | flops 12582912 | bytes 29380608 | tf_op jit(solution)/shard_map/add | solution.py:101
  147.5 9.0 %copy.96 = f32[512,4096]{0,1:T(8,128)} copy(f32[512,4096]{1,0:T(8,128)} %get-tuple-element.112) | data formatting | bytes 16777216 | tf_op jit(solution)/shard_map/add | solution.py:101
  156.6 9.0 %copy.97 = f32[512,4096]{0,1:T(8,128)} copy(f32[512,4096]{1,0:T(8,128)} %get-tuple-element.113) | data formatting | bytes 16777216 | tf_op jit(solution)/shard_map/mul | solution.py:101
  165.6 10.3 %add_convert_fusion = bf16[5,512,4096]{1,2,0:T(8,128)(2,1)S(1)} fusion(f32[5,4096]{1,0:T(8,128)S(1)} %slice.75, f32[512,4096]{0,1:T(8,128)} %copy.97, f32[512,4096]{0,1:T(8,128)} %copy.96), kind=kLoop, calls=%fused_computation.28 | loop fusion | flops 31457280 | bytes 37830656 | tf_op jit(solution)/shard_map/convert_element_type | solution.py:101
  175.9 6.5 slice.77
  182.4 4.2 copy-done.4
  186.7 12.8 %gather_fusion = bf16[128,3,512,32]{2,3,1,0:T(8,128)(2,1)} fusion(bf16[3,512,128,32]{1,3,2,0:T(8,128)(2,1)} %bitcast.253, s32[1024]{0:T(1024)S(1)} %pad_clamp_fusion), kind=kCustom, calls=%fused_computation | custom fusion | bytes 25166336 | tf_op jit(solution)/shard_map/jit(_take)/gather | solution.py:104
  199.5 10.7 %copy.98 = bf16[3,512,128,32]{1,3,2,0:T(8,128)(2,1)} copy(bf16[3,512,128,32]{1,3,0,2:T(8,128)(2,1)} %bitcast.254) | data formatting | bytes 25165824 | tf_op jit(solution)/shard_map/jit(_take)/gather | solution.py:104
  211.1 3.9 fusion.34
  217.7 11.7 %bitcast_select_fusion = bf16[3,512,4096]{1,2,0:T(8,128)(2,1)} fusion(bf16[3,512,128,32]{1,3,2,0:T(8,128)(2,1)} %copy.98, pred[4096]{0:T(1024)(128)(4,1)S(1)} %broadcast_in_dim.95), kind=kLoop, calls=%fused_computation.30 | loop fusion | flops 6291456 | bytes 25169920 | tf_op jit(solution)/shard_map/jit(_take)/select_n | solution.py:104
  231.9 6.5 copy.99
  238.4 11.9 %fusion.77 = f32[3,512,256]{2,1,0:T(8,128)} fusion(bf16[3,512,4096]{1,2,0:T(8,128)(2,1)} %bitcast_select_fusion, bf16[3,4096,256]{2,1,0:T(8,128)(2,1)} %bitcast.257), kind=kOutput, calls=%fused_computation.151 | convolution fusion | flops 3221225472 | bytes 20447232 | tf_op jit(solution)/shard_map/mtd,mdc->mtc/dot_general | solution.py:128
  250.3 2.6 fusion.74
  254.4 2.5 reshape_squeeze.6
  256.9 2.4 reshape_squeeze.7
  260.8 79.8 %while.12 = (s32[]{:T(128)}, f32[4,64,64]{2,1,0:T(8,128)S(1)}, f32[8,64,4,64]{3,1,2,0:T(8,128)}, f32[8,64,4,64]{3,2,1,0:T(4,128)}, f32[8,64,4,64]{3,2,1,0:T(4,12...) while((s32[]{:T(128)}, f32[4,64,64]{2,1,0:T(8,128)S(1)}, ...), condition=%wide.region_6.7_spmd, body=%wide.region_2.6_spmd.sunk | while | flops 45260544 | bytes 2537577 | solution.py:159
  264.7 3.4 multiply_reduce_fusion.6
  274.7 3.4 multiply_reduce_fusion.6
  284.6 3.4 multiply_reduce_fusion.6
  294.6 3.4 multiply_reduce_fusion.6
  304.5 3.4 multiply_reduce_fusion.6
  314.5 3.4 multiply_reduce_fusion.6
  324.5 3.4 multiply_reduce_fusion.6
  334.4 3.4 multiply_reduce_fusion.6
  340.6 2.0 copy.103
  345.7 1.9 multiply_reduce_fusion.2
  349.0 9.6 %convolution_convert_fusion.1 = bf16[512,4096]{1,0:T(8,128)(2,1)} fusion(bf16[256,4096]{1,0:T(8,128)(2,1)S(1)} %copy-done, bf16[4096,256]{1,0:T(8,128)(2,1)} %param.39, bf16[5,512,4096]{1,2,0:T(8,128)(2,1)} %copy-done.4, f32[512,256]{1,0:T(8,128)S(1)} %copy.108, f32[512,256]{1,0:T(8,128)} %reshape.248, f32[512,256]{1,0:T(8,128)} %copy.105, ...), kind=kOutput, calls=%fused_computation.54 | convolution fusion | flops 2150760448 | bytes 14156800 | tf_op jit(solution)/shard_map/dot_general | solution.py:165
  360.0 129.4 %all-reduce.2.cloned.1.call-done = bf16[512,4096]{1,0:T(8,128)(2,1)} async-done(((bf16[512,4096]{1,0:T(8,128)(2,1)}), bf16[512,4096]{1,0:T(8,128)(2,1)}) %all-reduce.2.cloned.1.call-update) | async-done | bytes 4194320 | tf_op jit(solution)/shard_map/psum | solution.py:166
  489.4 5.2 convert_reduce_fusion.1
  495.8 2.1 fusion.22
  497.9 3.5 maximum_subtract_fusion.1
  501.4 4.8 add_convert_fusion.1
  506.2 83.5 %all-gather.6.cloned.1.call-done = bf16[896,4096]{1,0:T(8,128)(2,1)} async-done(((bf16[112,4096]{1,0:T(8,128)(2,1)}), bf16[896,4096]{1,0:T(8,128)(2,1)}) %all-gather.6.cloned.1.call-update) | async-done | bytes 7340048 | tf_op jit(solution)/shard_map/all_gather | solution.py:176
  589.7 99.4 %all-gather.8.cloned.1.call-done = bf16[896,4096]{1,0:T(8,128)(2,1)} async-done(((bf16[112,4096]{1,0:T(8,128)(2,1)}), bf16[896,4096]{1,0:T(8,128)(2,1)}) %all-gather.8.cloned.1.call-update) | async-done | bytes 7340048 | tf_op jit(solution)/shard_map/all_gather | solution.py:177
  689.1 16.2 %convolution_convert_fusion = bf16[512,4096]{1,0:T(8,128)(2,1)} fusion(bf16[896,4096]{1,0:T(8,128)(2,1)} %all-gather.8.cloned.1.call-done, bf16[896,4096]{1,0:T(8,128)(2,1)} %all-gather.6.cloned.1.call-done, bf16[2,512,4096]{2,1,0:T(8,128)(2,1)} %add_convert_fusion.1), kind=kOutput, calls=%fused_computation.53 | convolution fusion | flops 7519666176 | bytes 23068672 | tf_op jit(solution)/shard_map/dot_general | solution.py:182
  707.8 64.5 %reduce-scatter.2.cloned.1.call-done = bf16[512,256]{1,0:T(8,128)(2,1)} async-done(((bf16[512,4096]{1,0:T(8,128)(2,1)}), bf16[512,256]{1,0:T(8,128)(2,1)}) %reduce-scatter.2.cloned.1.call-update) | async-done | bytes 262160 | tf_op jit(solution)/shard_map/reduce_scatter | solution.py:183
  772.3 4.9 fusion.45
  (215 shorter events, 100.3 us)
Async XLA Ops:
  7.2 341.8 %copy-start = (bf16[256,4096]{1,0:T(8,128)(2,1)S(1)}, bf16[256,4096]{1,0:T(8,128)(2,1)}, u32[]{:S(2)}) copy-start(bf16[256,4096]{1,0:T(8,128)(2,1)} %param.40) | copy-start | bytes 6291460
  7.2 14.1 %copy-start.11 = (bf16[1,2,4096]{2,1,0:T(2,128)(2,1)S(1)}, bf16[1,2,4096]{2,1,0:T(2,128)(2,1)}, u32[]{:S(2)}) copy-start(bf16[1,2,4096]{2,1,0:T(2,128)(2,1)} %param.42) | copy-start | bytes 49156
  7.2 96.5 %all-gather.4.cloned.1.call-start = ((), (), s32[]{:S(2)}) async-start(), calls=%async_computation.3 | async-start | bytes 7077888 | tf_op jit(solution)/shard_map/all_gather | solution.py:110
  10.7 17.5 %copy-start.9 = (bf16[2,4096]{1,0:T(2,128)(2,1)S(1)}, bf16[2,4096]{1,0:T(2,128)(2,1)}, u32[]{:S(2)}) copy-start(bf16[2,4096]{1,0:T(2,128)(2,1)} %param.32) | copy-start | bytes 49156
  14.0 118.2 %all-to-all-start = ((bf16[16,2,8192]{2,1,0:T(2,128)(2,1)}), bf16[16,2,8192]{2,1,0:T(2,128)(2,1)S(1)}, u32[]{:S(2)}, u32[]{:S(2)}) async-start(bf16[16,2,8192]{2,1,0:T(2,128)(2,1)} %reshape.259), calls=%async_computation | async-start | bytes 1048576 | tf_op jit(solution)/shard_map/all_to_all | solution.py:139
  20.4 8.4 %copy-start.1 = (bf16[1,512,4096]{2,1,0:T(8,128)(2,1)S(1)}, bf16[1,512,4096]{2,1,0:T(8,128)(2,1)}, u32[]{:S(2)}) copy-start(bf16[1,512,4096]{2,1,0:T(8,128)(2,1)} %param.24) | copy-start | bytes 12582916
  30.7 3.3 copy-start.5
  132.2 99.8 %all-to-all-start.1 = ((bf16[16,3,256,256]{3,2,1,0:T(8,128)(2,1)}), bf16[16,3,256,256]{3,2,1,0:T(8,128)(2,1)}, u32[]{:S(2)}, u32[]{:S(2)}) async-start(bf16[16,3,256,256]{3,2,1,0:T(8,128)(2,1)} %fusion.49), calls=%async_computation.1 | async-start | bytes 12582912 | tf_op jit(solution)/shard_map/all_to_all | solution.py:112
  136.8 352.5 %all-reduce.2.cloned.1.call-start = ((), (), s32[]{:S(2)}) async-start(), calls=%async_computation.4 | async-start | bytes 8388608 | tf_op jit(solution)/shard_map/psum | solution.py:166
  156.6 9.0 %copy-start.7 = (bf16[7,4096]{1,0:T(8,128)(2,1)S(1)}, bf16[7,4096]{1,0:T(8,128)(2,1)}, u32[]{:S(2)}) copy-start(bf16[7,4096]{1,0:T(8,128)(2,1)} %param.33) | copy-start | bytes 172036
  175.9 10.7 %copy-start.4 = (bf16[5,512,4096]{1,2,0:T(8,128)(2,1)}, bf16[5,512,4096]{1,2,0:T(8,128)(2,1)S(1)}, u32[]{:S(2)}) copy-start(bf16[5,512,4096]{1,2,0:T(8,128)(2,1)S(1)} %add_convert_fusion) | copy-start | bytes 62914564
  175.9 10.7 %copy-start.16 = (s32[128]{0:T(128)S(1)}, s32[128]{0:T(128)}, u32[]{:S(2)}) copy-start(s32[128]{0:T(128)} %param.28) | copy-start | bytes 1540
  199.5 11.6 %copy-start.13 = (bf16[128,256]{1,0:T(8,128)(2,1)S(1)}, bf16[128,256]{1,0:T(8,128)(2,1)}, u32[]{:S(2)}) copy-start(bf16[128,256]{1,0:T(8,128)(2,1)} %param.36) | copy-start | bytes 196612
  199.5 11.6 %copy-start.14 = (f32[256]{0:T(256)S(1)}, f32[256]{0:T(256)}, u32[]{:S(2)}) copy-start(f32[256]{0:T(256)} %param.34) | copy-start | bytes 3076
  211.1 18.3 %copy-start.17 = (pred[512]{0:T(512)(128)(4,1)}, pred[512]{0:T(512)(128)(4,1)S(1)}, u32[]{:S(2)}) copy-start(pred[512]{0:T(512)(128)(4,1)S(1)} %iota_compare_fusion.1) | copy-start | bytes 1540
  250.3 8.9 %copy-start.12 = (pred[8,64]{1,0:T(8,128)(4,1)S(1)}, pred[8,64]{1,0:T(8,128)(4,1)}, u32[]{:S(2)}) copy-start(pred[8,64]{1,0:T(8,128)(4,1)} %add_compare_fusion) | copy-start | bytes 1540
  340.6 18.0 %copy-start.6 = (f32[4,64,64]{2,1,0:T(8,128)}, f32[4,64,64]{2,1,0:T(8,128)S(1)}, u32[]{:S(2)}) copy-start(f32[4,64,64]{2,1,0:T(8,128)S(1)} %get-tuple-element.47) | copy-start | bytes 196612
  340.6 8.4 %copy-start.15 = (f32[256]{0:T(256)S(1)}, f32[256]{0:T(256)}, u32[]{:S(2)}) copy-start(f32[256]{0:T(256)} %param.38) | copy-start | bytes 3076
  349.0 11.0 %copy-start.8 = (bf16[7,4096]{1,0:T(8,128)(2,1)S(1)}, bf16[7,4096]{1,0:T(8,128)(2,1)}, u32[]{:S(2)}) copy-start(bf16[7,4096]{1,0:T(8,128)(2,1)} %param.33) | copy-start | bytes 172036
  358.6 231.1 %all-gather.6.cloned.1.call-start = ((), (), s32[]{:S(2)}) async-start(), calls=%async_computation.5 | async-start | bytes 8257536 | tf_op jit(solution)/shard_map/all_gather | solution.py:176
  359.3 329.8 %all-gather.8.cloned.1.call-start = ((), (), s32[]{:S(2)}) async-start(), calls=%async_computation.6 | async-start | bytes 8257536 | tf_op jit(solution)/shard_map/all_gather | solution.py:177
  359.9 412.4 %reduce-scatter.2.cloned.1.call-start = ((), (), s32[]{:S(2)}) async-start(), calls=%async_computation.7 | async-start | bytes 4456448 | tf_op jit(solution)/shard_map/reduce_scatter | solution.py:183
  494.5 3.4 copy-start.3
  495.8 2.2 copy-start.10
  497.9 3.5 copy-start.2
  506.2 266.1 %copy-start.18 = (pred[512]{0:T(512)(128)(4,1)S(1)}, pred[512]{0:T(512)(128)(4,1)}, u32[]{:S(2)}) copy-start(pred[512]{0:T(512)(128)(4,1)} %copy-done.17) | copy-start | bytes 1540
Sparse Core Ops, SparseCore 0:
  10.8 92.8 all-gather.3
  358.7 130.5 all-reduce.1
  491.7 97.9 all-gather.5
  591.9 97.1 all-gather.7
  705.4 66.8 reduce-scatter.1
